TPU v7x, 32 devices: a whole 2x2x4 slice. The times are simulated.
32 devices in a mesh: dp: 4 (over z), seq: 8 (over y, x, core).
Axes of the slice: x: 2, y: 2, z: 4, core: 2. Of those that a mesh axis runs over, the one named last changes fastest.
Arguments:
- hidden: bfloat16 [8, 2048, 1536], P('dp', 'seq'), may hold values from -8 to 8
- lengths: int32 [8], P('dp'), may hold values from 1024 to 2048, as said below
- cotangent: bfloat16 [8, 2048, 1536], P('dp', 'seq'), may hold values from -6 to 6
- norm_gain: bfloat16 [2, 1536], P(None, 'dp'), may hold values from 0.5 to 1.5
- in_weight: bfloat16 [2, 1536, 6448], P(None, 'dp'), may hold values from -0.15625 to 0.15625
- conv_weight: bfloat16 [2, 4, 3328], P(None, None, 'dp'), may hold values from -3 to 3
- conv_bias: bfloat16 [2, 3328], P(None, 'dp'), may hold values from -1.5 to 1.5
- dt_bias: bfloat16 [2, 48], P(None, 'dp'), may hold values from -9 to -3
- decay_log: bfloat16 [2, 48], P(None, 'dp'), may hold values from -1 to 1.5
- skip_gain: bfloat16 [2, 48], P(None, 'dp'), may hold values from 0.5 to 2
- gate_gain: bfloat16 [2, 3072], P(None, 'dp'), may hold values from 0.5 to 1.5
- out_weight: bfloat16 [2, 3072, 1536], P(None, 'dp'), may hold values from -0.109375 to 0.109375
Outputs:
- output: float32 [8, 2048, 1536], P('dp', 'seq')
- grad_hidden: float32 [8, 2048, 1536], P('dp', 'seq')
- grad_norm_gain: float32 [2, 1536], P(None, 'dp')
- grad_in_weight: float32 [2, 1536, 6448], P(None, 'dp')
- grad_conv_weight: float32 [2, 4, 3328], P(None, None, 'dp')
- grad_conv_bias: float32 [2, 3328], P(None, 'dp')
- grad_dt_bias: float32 [2, 48], P(None, 'dp')
- grad_decay_log: float32 [2, 48], P(None, 'dp')
- grad_skip_gain: float32 [2, 48], P(None, 'dp')
- grad_gate_gain: float32 [2, 3072], P(None, 'dp')
- grad_out_weight: float32 [2, 3072, 1536], P(None, 'dp')
- norm_stats: float32 [2, 2], replicated
Inputs may be any that keep to these rules, and one draw needn't show every extreme that they name: Sequence s has valid slots 0 .. lengths[s] - 1; in every draw one sequence has all 2048 slots valid and another exactly 1024.
All inputs are finite; a program needn't handle non-finite values.
Results may differ from a plain program's by a relative error of at most 0.02.
Values may be sent and summed in bfloat16 or wider, within the bound.
A program may use at most 576 MiB of HBM per device.

v0:
```python
import jax
import jax.numpy as jnp
from jax import lax
from jax.sharding import PartitionSpec as P

D = 1536
HEADS = 48
HEAD_DIM = 64
STATE = 128
CONV = 4
BLOCK = 256
LAYERS = 2
DIN = 3072


epsilon = 1e-05
highest = lax.Precision.HIGHEST


def norm_rows(values, scales):
    return values * lax.rsqrt(jnp.mean(values * values, -1, keepdims=True) + epsilon) * scales


def causal(values, kernel, offset):
    length = values.shape[-2]
    widths = [(0, 0)] * (values.ndim - 2) + [(kernel.shape[0] - 1, 0), (0, 0)]
    padded = jnp.pad(values, widths)
    running = jnp.expand_dims(offset, -2)
    for tap_index in range(kernel.shape[0]):
        running = (
            running
            + jnp.expand_dims(kernel[tap_index], -2)
            * padded[..., tap_index : tap_index + length, :]
        )
    return running


def prepare(x_raw, bc_raw, step_raw, conv_x, bias_x, conv_bc, bias_bc, step_offset, decay_rate):
    x_active = jax.nn.silu(causal(x_raw, conv_x, bias_x))
    bc_active = jax.nn.silu(causal(bc_raw, conv_bc, bias_bc))
    step_sizes = jax.nn.softplus(step_raw + step_offset[:, None])
    log_decay = -step_sizes * jnp.exp(decay_rate)[:, None]
    cumulative = jnp.cumsum(log_decay.reshape(log_decay.shape[0], -1, BLOCK), -1)
    return (x_active, bc_active, step_sizes, cumulative)


def weigh_block(scores, cumulative, step_sizes):
    block_size = cumulative.shape[-1]
    lower_mask = jnp.arange(block_size)[:, None] >= jnp.arange(block_size)[None, :]
    spread = cumulative[..., :, None] - cumulative[..., None, :]
    decay = jnp.where(lower_mask, jnp.exp(jnp.where(lower_mask, spread, 0.0)), 0.0)
    return scores * decay * step_sizes[..., None, :]


def across(values, write_rows, read_rows, step_sizes, cumulative, skip_scale):
    totals = cumulative[..., -1]
    weights = jnp.exp(totals[..., None] - cumulative) * step_sizes
    weighted = weights[..., None] * values
    states = jnp.einsum("kbjp,bjn->kbpn", weighted, write_rows, precision=highest)
    block_ends = jnp.cumsum(totals, -1)
    starts = block_ends - totals
    block_count = totals.shape[-1]
    before_mask = jnp.arange(block_count)[:, None] > jnp.arange(block_count)[None, :]
    spread = starts[..., :, None] - block_ends[..., None, :]
    carried_decay = jnp.where(before_mask, jnp.exp(jnp.where(before_mask, spread, 0.0)), 0.0)
    entering = jnp.einsum("kcd,kdpn->kcpn", carried_decay, states, precision=highest)
    readout = jnp.einsum("bin,kbpn->kbip", read_rows, entering, precision=highest)
    return jnp.exp(cumulative)[..., None] * readout + skip_scale[:, None, None, None] * values


def gated_norm(values, gate_in, scales):
    gated = values * jax.nn.silu(gate_in)
    return gated * lax.rsqrt(jnp.mean(gated * gated, -1, keepdims=True) + epsilon) * scales


def shard_of(whole_array, rank_total, rank_index, axis_dim):
    piece_len = whole_array.shape[axis_dim] // rank_total
    return lax.dynamic_slice_in_dim(whole_array, rank_index * piece_len, piece_len, axis_dim)


def local(
    hidden,
    lengths,
    cotangent,
    norm_gain,
    in_weight,
    conv_weight,
    conv_bias,
    dt_bias,
    decay_log,
    skip_gain,
    gate_gain,
    out_weight,
):
    seq_total = lax.axis_size("seq")
    seq_rank = lax.axis_index("seq")
    data_total = lax.axis_size("dp")
    data_rank = lax.axis_index("dp")
    local_seqs = hidden.shape[0]
    row_count = hidden.shape[1]
    slot_count = row_count * seq_total
    blocks = slot_count // BLOCK
    item_count = local_seqs * HEADS // seq_total
    copies = seq_total // local_seqs
    first_head = seq_rank * item_count % HEADS
    positions = seq_rank * row_count + jnp.arange(row_count)
    valid_mask = (positions[None, :] < lengths[:, None]).astype(jnp.float32)
    hidden_now = hidden.astype(jnp.float32)
    kept_layers = []
    squares = []
    for layer_index in range(LAYERS):
        weights = (
            lax.all_gather(norm_gain[layer_index], "dp", axis=0, tiled=True),
            lax.all_gather(in_weight[layer_index], "dp", axis=0, tiled=True),
            lax.all_gather(conv_weight[layer_index], "dp", axis=1, tiled=True),
            lax.all_gather(conv_bias[layer_index], "dp", axis=0, tiled=True),
            lax.all_gather(dt_bias[layer_index], "dp", axis=0, tiled=True),
            lax.all_gather(decay_log[layer_index], "dp", axis=0, tiled=True),
            lax.all_gather(skip_gain[layer_index], "dp", axis=0, tiled=True),
            lax.all_gather(gate_gain[layer_index], "dp", axis=0, tiled=True),
            lax.all_gather(out_weight[layer_index], "dp", axis=0, tiled=True),
        )
        (
            norm_scale,
            proj_in,
            conv_kernel,
            conv_offset,
            step_offset,
            decay_rate,
            skip_scale,
            gate_scale,
            proj_out,
        ) = weights
        normed, norm_pull = jax.vjp(norm_rows, hidden_now, norm_scale.astype(jnp.float32))
        normed_low = normed.astype(jnp.bfloat16)
        proj_gate = proj_in[:, :DIN]
        proj_x = proj_in[:, DIN : 2 * DIN].reshape(D, HEADS, HEAD_DIM)
        proj_bc = proj_in[:, 2 * DIN : 2 * DIN + 2 * STATE]
        proj_step = proj_in[:, 2 * DIN + 2 * STATE :]
        gate_in = jnp.einsum(
            "std,df->stf", normed_low, proj_gate, preferred_element_type=jnp.float32
        )
        x_send = (
            jnp.einsum("std,dhp->shtp", normed_low, proj_x, preferred_element_type=jnp.float32)
            .astype(jnp.bfloat16)
            .reshape(local_seqs * HEADS, row_count // 2, 2 * HEAD_DIM)
        )
        step_send = (
            jnp.einsum("std,dh->sht", normed_low, proj_step, preferred_element_type=jnp.float32)
            .astype(jnp.bfloat16)
            .reshape(local_seqs * HEADS, row_count)
        )
        bc_local = jnp.einsum(
            "std,dc->stc", normed_low, proj_bc, preferred_element_type=jnp.float32
        ).astype(jnp.bfloat16)
        bc_send = jnp.repeat(bc_local, copies, axis=0)
        x_heads, step_heads, bc_heads = (
            lax.all_to_all(x_send, "seq", split_axis=0, concat_axis=1, tiled=True),
            lax.all_to_all(step_send, "seq", split_axis=0, concat_axis=1, tiled=True),
            lax.all_to_all(bc_send, "seq", split_axis=0, concat_axis=1, tiled=True),
        )
        conv_x = (
            lax.dynamic_slice_in_dim(
                conv_kernel[:, :DIN], first_head * HEAD_DIM, item_count * HEAD_DIM, 1
            )
            .astype(jnp.float32)
            .reshape(CONV, item_count, HEAD_DIM)
        )
        bias_x = (
            lax.dynamic_slice_in_dim(
                conv_offset[:DIN], first_head * HEAD_DIM, item_count * HEAD_DIM, 0
            )
            .astype(jnp.float32)
            .reshape(item_count, HEAD_DIM)
        )
        head_offset = lax.dynamic_slice_in_dim(step_offset, first_head, item_count, 0).astype(
            jnp.float32
        )
        head_rate = lax.dynamic_slice_in_dim(decay_rate, first_head, item_count, 0).astype(
            jnp.float32
        )
        head_skip = lax.dynamic_slice_in_dim(skip_scale, first_head, item_count, 0).astype(
            jnp.float32
        )
        prepared, prep_pull = jax.vjp(
            prepare,
            x_heads.reshape(item_count, slot_count, HEAD_DIM).astype(jnp.float32),
            bc_heads[0].astype(jnp.float32),
            step_heads.astype(jnp.float32),
            conv_x,
            bias_x,
            conv_kernel[:, DIN:].astype(jnp.float32),
            conv_offset[DIN:].astype(jnp.float32),
            head_offset,
            head_rate,
        )
        x_active, bc_active, step_sizes, cumulative = prepared
        x_low = x_active.astype(jnp.bfloat16).reshape(item_count, blocks, BLOCK, HEAD_DIM)
        write_low = bc_active[:, :STATE].astype(jnp.bfloat16).reshape(blocks, BLOCK, STATE)
        read_low = bc_active[:, STATE:].astype(jnp.bfloat16).reshape(blocks, BLOCK, STATE)
        step_blocks = step_sizes.reshape(item_count, blocks, BLOCK)
        scores = jnp.einsum("bin,bjn->bij", read_low, write_low, preferred_element_type=jnp.float32)
        mixing = weigh_block(scores, cumulative, step_blocks)
        mixing_low = mixing.astype(jnp.bfloat16)
        direct = jnp.einsum(
            "kbij,kbjp->kbip", mixing_low, x_low, preferred_element_type=jnp.float32
        )
        carried, across_pull = jax.vjp(
            across,
            x_low.astype(jnp.float32),
            write_low.astype(jnp.float32),
            read_low.astype(jnp.float32),
            step_blocks,
            cumulative,
            head_skip,
        )
        heads_out = (
            (direct + carried)
            .astype(jnp.bfloat16)
            .reshape(item_count, slot_count // 2, 2 * HEAD_DIM)
        )
        back_tokens = lax.all_to_all(heads_out, "seq", split_axis=1, concat_axis=0, tiled=True)
        y_tokens = (
            back_tokens.reshape(local_seqs, HEADS, row_count, HEAD_DIM)
            .transpose(0, 2, 1, 3)
            .reshape(local_seqs, row_count, DIN)
            .astype(jnp.float32)
        )
        gated_out, gate_pull = jax.vjp(
            gated_norm, y_tokens, gate_in, gate_scale.astype(jnp.float32)
        )
        gated_low = gated_out.astype(jnp.bfloat16)
        mixer_out = jnp.einsum(
            "stf,fd->std", gated_low, proj_out, preferred_element_type=jnp.float32
        )
        squares.append(jnp.sum(hidden_now * hidden_now * valid_mask[..., None]))
        squares.append(jnp.sum(mixer_out * mixer_out * valid_mask[..., None]))
        kept_layers.append(
            (
                normed_low,
                norm_pull,
                prep_pull,
                x_low,
                write_low,
                read_low,
                mixing_low,
                (scores, cumulative, step_blocks),
                across_pull,
                gate_pull,
                gated_low,
                weights,
            )
        )
        hidden_now = hidden_now + mixer_out
    output = hidden_now * valid_mask[..., None]
    square_sums, valid_total = lax.psum((jnp.stack(squares), jnp.sum(valid_mask)), ("dp", "seq"))
    norm_stats = jnp.sqrt(square_sums.reshape(LAYERS, 2) / (valid_total * D))
    grad_state = cotangent.astype(jnp.float32) * valid_mask[..., None]
    collected = [None] * LAYERS
    large_in = [None] * LAYERS
    large_out = [None] * LAYERS
    for layer_index in reversed(range(LAYERS)):
        (
            normed_low,
            norm_pull,
            prep_pull,
            x_low,
            write_low,
            read_low,
            mixing_low,
            weigh_kept,
            across_pull,
            gate_pull,
            gated_low,
            weights,
        ) = kept_layers[layer_index]
        unused_mixing, weigh_pull = jax.vjp(
            weigh_block, weigh_kept[0], weigh_kept[1], weigh_kept[2]
        )
        proj_in = weights[1]
        proj_out = weights[8]
        grad_low = grad_state.astype(jnp.bfloat16)
        grad_proj_out = jnp.einsum(
            "stf,std->fd", gated_low, grad_low, preferred_element_type=jnp.float32
        )
        grad_gated = jnp.einsum(
            "std,fd->stf", grad_low, proj_out, preferred_element_type=jnp.float32
        )
        grad_y, grad_gate_in, grad_gate_scale = gate_pull(grad_gated)
        grad_y_send = (
            grad_y.astype(jnp.bfloat16)
            .reshape(local_seqs, row_count, HEADS, HEAD_DIM)
            .transpose(0, 2, 1, 3)
            .reshape(local_seqs * HEADS, row_count // 2, 2 * HEAD_DIM)
        )
        grad_heads = lax.all_to_all(
            grad_y_send, "seq", split_axis=0, concat_axis=1, tiled=True
        ).reshape(item_count, blocks, BLOCK, HEAD_DIM)
        grad_x_c, grad_write_c, grad_read_c, grad_steps_c, grad_cum_c, grad_skip = across_pull(
            grad_heads.astype(jnp.float32)
        )
        grad_mixing = jnp.einsum(
            "kbip,kbjp->kbij", grad_heads, x_low, preferred_element_type=jnp.float32
        )
        grad_x_d = jnp.einsum(
            "kbij,kbip->kbjp", mixing_low, grad_heads, preferred_element_type=jnp.float32
        )
        grad_scores, grad_cum_d, grad_steps_d = weigh_pull(grad_mixing)
        grad_read_d = jnp.einsum(
            "bij,bjn->bin", grad_scores, write_low.astype(jnp.float32), precision=highest
        )
        grad_write_d = jnp.einsum(
            "bij,bin->bjn", grad_scores, read_low.astype(jnp.float32), precision=highest
        )
        grad_bc_active = jnp.concatenate(
            [
                (grad_write_c + grad_write_d).reshape(slot_count, STATE),
                (grad_read_c + grad_read_d).reshape(slot_count, STATE),
            ],
            1,
        )
        pulled = prep_pull(
            (
                (grad_x_c + grad_x_d).reshape(item_count, slot_count, HEAD_DIM),
                grad_bc_active,
                (grad_steps_c + grad_steps_d).reshape(item_count, slot_count),
                grad_cum_c + grad_cum_d,
            )
        )
        (
            grad_x_raw,
            grad_bc_raw,
            grad_step_raw,
            grad_conv_x,
            grad_bias_x,
            grad_conv_bc,
            grad_bias_bc,
            grad_offset,
            grad_rate,
        ) = pulled
        x_back, step_back = (
            lax.all_to_all(
                grad_x_raw.astype(jnp.bfloat16).reshape(item_count, slot_count // 2, 2 * HEAD_DIM),
                "seq",
                split_axis=1,
                concat_axis=0,
                tiled=True,
            ),
            lax.all_to_all(
                grad_step_raw.astype(jnp.bfloat16), "seq", split_axis=1, concat_axis=0, tiled=True
            ),
        )
        bc_parts = lax.all_to_all(
            grad_bc_raw[None].astype(jnp.bfloat16), "seq", split_axis=1, concat_axis=0, tiled=True
        ).astype(jnp.float32)
        grad_bc = jnp.sum(bc_parts.reshape(local_seqs, copies, row_count, 2 * STATE), 1).astype(
            jnp.bfloat16
        )
        grad_x_tokens = (
            x_back.reshape(local_seqs, HEADS, row_count, HEAD_DIM)
            .transpose(0, 2, 1, 3)
            .reshape(local_seqs, row_count, DIN)
        )
        grad_step_tokens = step_back.reshape(local_seqs, HEADS, row_count).transpose(0, 2, 1)
        grad_proj_low = jnp.concatenate(
            [grad_gate_in.astype(jnp.bfloat16), grad_x_tokens, grad_bc, grad_step_tokens], 2
        )
        grad_proj_in = jnp.einsum(
            "std,stf->df", normed_low, grad_proj_low, preferred_element_type=jnp.float32
        )
        grad_normed = jnp.einsum(
            "stf,df->std", grad_proj_low, proj_in, preferred_element_type=jnp.float32
        )
        grad_input, grad_norm_scale = norm_pull(grad_normed)
        grad_state = grad_state + grad_input
        conv_whole = jnp.concatenate(
            [
                lax.dynamic_update_slice_in_dim(
                    jnp.zeros((CONV, DIN), jnp.float32),
                    grad_conv_x.reshape(CONV, item_count * HEAD_DIM),
                    first_head * HEAD_DIM,
                    1,
                ),
                grad_conv_bc,
            ],
            1,
        )
        bias_whole = jnp.concatenate(
            [
                lax.dynamic_update_slice_in_dim(
                    jnp.zeros((DIN,), jnp.float32),
                    grad_bias_x.reshape(item_count * HEAD_DIM),
                    first_head * HEAD_DIM,
                    0,
                ),
                grad_bias_bc,
            ],
            0,
        )
        offset_whole = lax.dynamic_update_slice_in_dim(
            jnp.zeros((HEADS,), jnp.float32), grad_offset, first_head, 0
        )
        rate_whole = lax.dynamic_update_slice_in_dim(
            jnp.zeros((HEADS,), jnp.float32), grad_rate, first_head, 0
        )
        skip_whole = lax.dynamic_update_slice_in_dim(
            jnp.zeros((HEADS,), jnp.float32), grad_skip, first_head, 0
        )
        summed = lax.psum(
            (
                grad_norm_scale,
                conv_whole,
                bias_whole,
                offset_whole,
                rate_whole,
                skip_whole,
                grad_gate_scale,
            ),
            ("dp", "seq"),
        )
        grad_parts = (
            lax.psum_scatter(
                grad_proj_in.astype(jnp.bfloat16), "dp", scatter_dimension=0, tiled=True
            ).astype(jnp.float32),
            lax.psum_scatter(
                grad_proj_out.astype(jnp.bfloat16), "dp", scatter_dimension=0, tiled=True
            ).astype(jnp.float32),
        )
        grad_large = (
            lax.psum(grad_parts[0].astype(jnp.bfloat16), "seq").astype(jnp.float32),
            lax.psum(grad_parts[1].astype(jnp.bfloat16), "seq").astype(jnp.float32),
        )
        large_in[layer_index] = grad_large[0]
        large_out[layer_index] = grad_large[1]
        collected[layer_index] = (
            shard_of(summed[0], data_total, data_rank, 0),
            shard_of(summed[1], data_total, data_rank, 1),
            shard_of(summed[2], data_total, data_rank, 0),
            shard_of(summed[3], data_total, data_rank, 0),
            shard_of(summed[4], data_total, data_rank, 0),
            shard_of(summed[5], data_total, data_rank, 0),
            shard_of(summed[6], data_total, data_rank, 0),
        )
    grad_in_stack = jnp.stack(large_in, 0)
    grad_out_stack = jnp.stack(large_out, 0)
    stacked = [
        jnp.stack([collected[layer_index][member] for layer_index in range(LAYERS)], 0)
        for member in range(7)
    ]
    return (
        output,
        grad_state,
        stacked[0],
        grad_in_stack,
        stacked[1],
        stacked[2],
        stacked[3],
        stacked[4],
        stacked[5],
        stacked[6],
        grad_out_stack,
        norm_stats,
    )


def solution(mesh):
    return jax.shard_map(
        local,
        mesh=mesh,
        in_specs=(
            P("dp", "seq", None),
            P("dp"),
            P("dp", "seq", None),
            P(None, "dp"),
            P(None, "dp", None),
            P(None, None, "dp"),
            P(None, "dp"),
            P(None, "dp"),
            P(None, "dp"),
            P(None, "dp"),
            P(None, "dp"),
            P(None, "dp", None),
        ),
        out_specs=(
            P("dp", "seq", None),
            P("dp", "seq", None),
            P(None, "dp"),
            P(None, "dp", None),
            P(None, None, "dp"),
            P(None, "dp"),
            P(None, "dp"),
            P(None, "dp"),
            P(None, "dp"),
            P(None, "dp"),
            P(None, "dp", None),
            P(),
        ),
        check_vma=False,
    )
```

profile of v0, /device:TPU:0, one launch (start us, length us, event | category | flops | bytes accessed | tf_op | source)
XLA Modules:
  0.0 3100.5 jit_solution(1862113132042168109)
XLA Ops:
  38.7 65.2 %all-gather.1 = bf16[1,4,3328]{1,0,2:T(2,128)(2,1)S(1)} all-gather(bf16[1,4,832]{1,0,2:T(2,128)(2,1)} %copy.717), channel_id=3, replica_groups=mesh['dp'=4,'seq'=8] {'dp'}, dimensions={2}, use_global_device_ids=true | all-gather | bytes 33280 | tf_op jit(solution)/shard_map/all_gather | solution.py:115
  109.5 46.1 %all-reduce.48 = (bf16[3328]{0:T(1024)(128)(2,1)S(1)}, bf16[48]{0:T(256)(128)(2,1)S(1)}, bf16[48]{0:T(256)(128)(2,1)S(1)}, bf16[48]{0:T(256)(128)(2,1)S(1)}, bf1...) all-reduce(bf16[3328]{0:T(1024)(128)(2,1)S(1)} %dynamic-update-slic, ...), channel_id=2, replica_groups=mesh['dp'=4,'seq'=8] {'dp'}, use_global_device_ids=true, to_apply=%add.38 | all-reduce | flops 6944 | bytes 27776
  183.7 59.3 %all-gather.10 = bf16[1,4,3328]{1,0,2:T(2,128)(2,1)S(1)} all-gather(bf16[1,4,832]{1,0,2:T(2,128)(2,1)} %copy.720), channel_id=12, replica_groups=mesh['dp'=4,'seq'=8] {'dp'}, dimensions={2}, use_global_device_ids=true | all-gather | bytes 33280 | tf_op jit(solution)/shard_map/all_gather | solution.py:115
  250.1 173.9 %all-gather.23.cloned.1.call-done = bf16[1,1536,6448]{2,1,0:T(8,128)(2,1)} async-done(((bf16[1,384,6448]{2,1,0:T(8,128)(2,1)}), bf16[1,1536,6448]{2,1,0:T(8,128)(2,1)}) %all-gather.23.cloned.1.call-update) | async-done | bytes 19808272 | tf_op jit(solution)/shard_map/all_gather | solution.py:114
  511.0 26.6 all-to-all-done.2
  551.9 30.0 multiply_convert_fusion.3
  680.4 86.2 %all-gather.27.cloned.1.call-done = bf16[1,1536,6448]{2,1,0:T(8,128)(2,1)} async-done(((bf16[1,384,6448]{2,1,0:T(8,128)(2,1)}), bf16[1,1536,6448]{2,1,0:T(8,128)(2,1)}) %all-gather.27.cloned.1.call-update) | async-done | bytes 19808272 | tf_op jit(solution)/shard_map/all_gather | solution.py:114
  834.4 99.8 %all-gather.25.cloned.1.call-done = bf16[1,3072,1536]{2,1,0:T(8,128)(2,1)} async-done(((bf16[1,768,1536]{2,1,0:T(8,128)(2,1)}), bf16[1,3072,1536]{2,1,0:T(8,128)(2,1)}) %all-gather.25.cloned.1.call-update) | async-done | bytes 9437200 | tf_op jit(solution)/shard_map/all_gather | solution.py:121
  1014.2 26.7 all-to-all-done.6
  1055.0 30.3 multiply_convert_fusion.2
  1156.1 35.9 %all-to-all-done.7 = bf16[12,1024,128]{2,0,1:T(8,128)(2,1)} async-done(((bf16[12,1024,128]{2,0,1:T(8,128)(2,1)}), bf16[12,1024,128]{2,0,1:T(8,128)(2,1)}, u32[]{:S(2)}, u32[]{:S(2)}) %all-to-all-start.7) | async-done | bytes 3145760 | tf_op jit(solution)/shard_map/all_to_all | solution.py:222
  1283.3 36.2 %all-to-all-done.8 = bf16[96,128,128]{2,1,0:T(8,128)(2,1)S(1)} async-done(((bf16[96,128,128]{2,1,0:T(8,128)(2,1)}), bf16[96,128,128]{2,1,0:T(8,128)(2,1)S(1)}, u32[]{:S(2)}, u32[]{:S(2)}) %all-to-all-start.8) | async-done | bytes 3145760 | tf_op jit(solution)/shard_map/all_to_all | solution.py:296
  1411.7 30.4 reduce-window.34
  1490.3 35.6 %multiply_reduce_fusion.7 = (f32[12,64]{1,0:T(8,128)}, f32[12,64]{1,0:T(8,128)}, f32[12,64]{1,0:T(8,128)}, f32[12,64]{1,0:T(8,128)}, f32[12,64]{1,0:T(8,128)}, /*index=5*/f32[12,2048,64]{2,1,0:T(8,128)}) fusion(f32[12,2048,64]{2,1,0:T(8,128)} %reshape.819, f32[12,2048,64]{2,1,0:T(8,128)} %get-tuple-element.117, f32[12,8,256,64]{3,2,1,0:T(8,128)} %copy.711), kind=kLoop, calls=%fused_computation.47 | loop fusion | flops 28307712 | bytes 25181184 | tf_op jit(solution)/shard_map/transpose(jvp())/reduce_sum | solution.py:32
  1609.1 44.0 %all-to-all-done.9 = bf16[12,1024,128]{2,0,1:T(8,128)(2,1)} async-done(((bf16[12,1024,128]{2,0,1:T(8,128)(2,1)}), bf16[12,1024,128]{2,0,1:T(8,128)(2,1)}, u32[]{:S(2)}, u32[]{:S(2)}) %all-to-all-start.9) | async-done | bytes 3145760 | tf_op jit(solution)/shard_map/all_to_all | solution.py:342
  1796.4 36.2 %all-to-all-done.12 = bf16[96,128,128]{2,1,0:T(8,128)(2,1)S(1)} async-done(((bf16[96,128,128]{2,1,0:T(8,128)(2,1)}), bf16[96,128,128]{2,1,0:T(8,128)(2,1)S(1)}, u32[]{:S(2)}, u32[]{:S(2)}) %all-to-all-start.12) | async-done | bytes 3145760 | tf_op jit(solution)/shard_map/all_to_all | solution.py:296
  1906.5 30.3 reduce-window.36
  2108.7 44.0 %all-to-all-done.13 = bf16[12,1024,128]{2,0,1:T(8,128)(2,1)} async-done(((bf16[12,1024,128]{2,0,1:T(8,128)(2,1)}), bf16[12,1024,128]{2,0,1:T(8,128)(2,1)}, u32[]{:S(2)}, u32[]{:S(2)}) %all-to-all-start.13) | async-done | bytes 3145760 | tf_op jit(solution)/shard_map/all_to_all | solution.py:342
  2188.3 24.5 copy.707
  2274.4 267.5 %reduce-scatter.13.cloned.1.call-done = bf16[384,6448]{1,0:T(8,128)(2,1)} async-done(((bf16[1536,6448]{1,0:T(8,128)(2,1)}), bf16[384,6448]{1,0:T(8,128)(2,1)}) %reduce-scatter.13.cloned.1.call-update) | async-done | bytes 4952080
  2549.4 158.0 %reduce-scatter.11.cloned.1.call-done = bf16[768,1536]{1,0:T(8,128)(2,1)} async-done(((bf16[3072,1536]{1,0:T(8,128)(2,1)}), bf16[768,1536]{1,0:T(8,128)(2,1)}) %reduce-scatter.11.cloned.1.call-update) | async-done | bytes 2359312 | tf_op jit(solution)/shard_map/reduce_scatter | solution.py:425
  2707.4 165.1 %reduce-scatter.9.cloned.1.call-done = bf16[768,1536]{1,0:T(8,128)(2,1)} async-done(((bf16[3072,1536]{1,0:T(8,128)(2,1)}), bf16[768,1536]{1,0:T(8,128)(2,1)}) %reduce-scatter.9.cloned.1.call-update) | async-done | bytes 2359312 | tf_op jit(solution)/shard_map/reduce_scatter | solution.py:425
  2908.2 46.5 %all-reduce.53 = (f32[1536]{0:T(1024)S(1)}, f32[1536]{0:T(1024)S(1)}, f32[4,3328]{1,0:T(4,128)S(1)}, f32[4,3328]{1,0:T(4,128)S(1)}, f32[3328]{0:T(1024)S(1)}, /*...) all-reduce(f32[1536]{0:T(1024)} %get-tuple-element.147, ...), channel_id=1, replica_groups=mesh['dp'=4,'seq'=8] {'dp','seq'}, use_global_device_ids=true, to_apply=%region_43.45 | all-reduce | flops 42789 | bytes 342312 | tf_op jit(solution)/shard_map/psum | solution.py:409
  2966.8 108.2 %all-reduce.52.cloned.1.call-done = (bf16[1,384,6448]{1,2,0:T(8,128)(2,1)}, bf16[1,384,6448]{1,2,0:T(8,128)(2,1)}, bf16[1,768,1536]{2,1,0:T(8,128)(2,1)}, bf16[1,768,1536]{2,1,0:T(8,128)(2,1)}) async-done(((bf16[1,384,6448]{1,2,0:T(8,128)(2,1)}, bf16[1,384,6448]{1,2,0:T(8,128)(2,1)}, bf16[1,768,1536]{2,1,0:T(8,128)(2,1)}, bf16[1,768,1536]{2,1,0:T(8,128)(2,1)}), (bf16[1,384,6448]{1,2,0:T(8,128)(2,1)}, ...) | async-done | bytes 14622736 | tf_op jit(solution)/shard_map/psum | solution.py:430
  (921 shorter events, 1374.3 us)
Async XLA Ops:
  7.2 416.8 %all-gather.23.cloned.1.call-start = ((), (), s32[]{:S(2)}) async-start(), calls=%async_computation.22 | async-start | bytes 25067520 | tf_op jit(solution)/shard_map/all_gather | solution.py:114
  23.5 743.0 %all-gather.27.cloned.1.call-start = ((), (), s32[]{:S(2)}) async-start(), calls=%async_computation.24 | async-start | bytes 25067520 | tf_op jit(solution)/shard_map/all_gather | solution.py:114
  31.3 903.0 %all-gather.25.cloned.1.call-start = ((), (), s32[]{:S(2)}) async-start(), calls=%async_computation.23 | async-start | bytes 11796480 | tf_op jit(solution)/shard_map/all_gather | solution.py:121
  426.3 28.7 all-to-all-start.1
  456.0 38.6 %all-to-all-start = ((bf16[8,256,256]{2,1,0:T(8,128)(2,1)}), bf16[8,256,256]{2,1,0:T(8,128)(2,1)S(1)}, u32[]{:S(2)}, u32[]{:S(2)}) async-start(bf16[8,256,256]{2,1,0:T(8,128)(2,1)} %bitcast.596), calls=%async_computation | async-start | bytes 2097152 | tf_op jit(solution)/shard_map/all_to_all | solution.py:160
  495.6 42.1 %all-to-all-start.2 = ((bf16[96,128,128]{2,1,0:T(8,128)(2,1)}), bf16[96,128,128]{2,1,0:T(8,128)(2,1)S(1)}, u32[]{:S(2)}, u32[]{:S(2)}) async-start(bf16[96,128,128]{2,1,0:T(8,128)(2,1)} %reshape.763), calls=%async_computation.2 | async-start | bytes 6291456 | tf_op jit(solution)/shard_map/all_to_all | solution.py:158
  635.3 152.7 %all-to-all-start.3 = ((bf16[12,1024,128]{2,0,1:T(8,128)(2,1)}), bf16[12,1024,128]{2,0,1:T(8,128)(2,1)}, u32[]{:S(2)}, u32[]{:S(2)}) async-start(bf16[12,1024,128]{2,0,1:T(8,128)(2,1)} %copy.526), calls=%async_computation.3 | async-start | bytes 8388608 | tf_op jit(solution)/shard_map/all_to_all | solution.py:222
  640.0 598.3 %all-gather.29.cloned.1.call-start = ((), (), s32[]{:S(2)}) async-start(), calls=%async_computation.25 | async-start | bytes 11796480 | tf_op jit(solution)/shard_map/all_gather | solution.py:121
  960.0 37.9 %all-to-all-start.4 = ((bf16[8,256,256]{2,1,0:T(8,128)(2,1)}), bf16[8,256,256]{2,1,0:T(8,128)(2,1)S(1)}, u32[]{:S(2)}, u32[]{:S(2)}) async-start(bf16[8,256,256]{2,1,0:T(8,128)(2,1)} %bitcast.597), calls=%async_computation.4 | async-start | bytes 2097152 | tf_op jit(solution)/shard_map/all_to_all | solution.py:160
  998.8 42.1 %all-to-all-start.6 = ((bf16[96,128,128]{2,1,0:T(8,128)(2,1)}), bf16[96,128,128]{2,1,0:T(8,128)(2,1)S(1)}, u32[]{:S(2)}, u32[]{:S(2)}) async-start(bf16[96,128,128]{2,1,0:T(8,128)(2,1)} %reshape.772), calls=%async_computation.6 | async-start | bytes 6291456 | tf_op jit(solution)/shard_map/all_to_all | solution.py:158
  1138.3 53.7 %all-to-all-start.7 = ((bf16[12,1024,128]{2,0,1:T(8,128)(2,1)}), bf16[12,1024,128]{2,0,1:T(8,128)(2,1)}, u32[]{:S(2)}, u32[]{:S(2)}) async-start(bf16[12,1024,128]{2,0,1:T(8,128)(2,1)} %copy.553), calls=%async_computation.7 | async-start | bytes 8388608 | tf_op jit(solution)/shard_map/all_to_all | solution.py:222
  1278.0 41.5 %all-to-all-start.8 = ((bf16[96,128,128]{2,1,0:T(8,128)(2,1)}), bf16[96,128,128]{2,1,0:T(8,128)(2,1)S(1)}, u32[]{:S(2)}, u32[]{:S(2)}) async-start(bf16[96,128,128]{2,1,0:T(8,128)(2,1)} %reshape.776), calls=%async_computation.8 | async-start | bytes 6291456 | tf_op jit(solution)/shard_map/all_to_all | solution.py:296
  1450.5 100.7 %all-to-all-start.11 = ((bf16[12,8,256]{2,0,1:T(8,128)(2,1)}), bf16[12,8,256]{2,0,1:T(8,128)(2,1)S(1)}, u32[]{:S(2)}, u32[]{:S(2)}) async-start(bf16[12,8,256]{2,0,1:T(8,128)(2,1)} %copy.592), calls=%async_computation.11 | async-start | bytes 131072 | tf_op jit(solution)/shard_map/all_to_all | solution.py:349
  1551.1 48.3 %all-to-all-start.10 = ((bf16[8,2,32768]{2,1,0:T(2,128)(2,1)}), bf16[8,2,32768]{2,1,0:T(2,128)(2,1)}, u32[]{:S(2)}, u32[]{:S(2)}) async-start(bf16[8,2,32768]{2,1,0:T(2,128)(2,1)} %reshape.987), calls=%async_computation.10 | async-start | bytes 2097152 | tf_op jit(solution)/shard_map/all_to_all | solution.py:353
  1599.4 53.7 %all-to-all-start.9 = ((bf16[12,1024,128]{2,0,1:T(8,128)(2,1)}), bf16[12,1024,128]{2,0,1:T(8,128)(2,1)}, u32[]{:S(2)}, u32[]{:S(2)}) async-start(bf16[12,1024,128]{2,0,1:T(8,128)(2,1)} %copy.571), calls=%async_computation.9 | async-start | bytes 8388608 | tf_op jit(solution)/shard_map/all_to_all | solution.py:342
  1603.9 662.6 %reduce-scatter.15.cloned.1.call-start = ((), (), s32[]{:S(2)}) async-start(), calls=%async_computation.27 | async-start | bytes 25067520
  1790.7 41.9 %all-to-all-start.12 = ((bf16[96,128,128]{2,1,0:T(8,128)(2,1)}), bf16[96,128,128]{2,1,0:T(8,128)(2,1)S(1)}, u32[]{:S(2)}, u32[]{:S(2)}) async-start(bf16[96,128,128]{2,1,0:T(8,128)(2,1)} %reshape.788), calls=%async_computation.12 | async-start | bytes 6291456 | tf_op jit(solution)/shard_map/all_to_all | solution.py:296
  1942.7 108.0 %all-to-all-start.15 = ((bf16[12,8,256]{2,0,1:T(8,128)(2,1)}), bf16[12,8,256]{2,0,1:T(8,128)(2,1)S(1)}, u32[]{:S(2)}, u32[]{:S(2)}) async-start(bf16[12,8,256]{2,0,1:T(8,128)(2,1)} %copy.632), calls=%async_computation.15 | async-start | bytes 131072 | tf_op jit(solution)/shard_map/all_to_all | solution.py:349
  2050.7 48.3 %all-to-all-start.14 = ((bf16[8,2,32768]{2,1,0:T(2,128)(2,1)}), bf16[8,2,32768]{2,1,0:T(2,128)(2,1)}, u32[]{:S(2)}, u32[]{:S(2)}) async-start(bf16[8,2,32768]{2,1,0:T(2,128)(2,1)} %reshape.989), calls=%async_computation.14 | async-start | bytes 2097152 | tf_op jit(solution)/shard_map/all_to_all | solution.py:353
  2099.0 53.7 %all-to-all-start.13 = ((bf16[12,1024,128]{2,0,1:T(8,128)(2,1)}), bf16[12,1024,128]{2,0,1:T(8,128)(2,1)}, u32[]{:S(2)}, u32[]{:S(2)}) async-start(bf16[12,1024,128]{2,0,1:T(8,128)(2,1)} %copy.611), calls=%async_computation.13 | async-start | bytes 8388608 | tf_op jit(solution)/shard_map/all_to_all | solution.py:342
  2103.6 438.3 %reduce-scatter.13.cloned.1.call-start = ((), (), s32[]{:S(2)}) async-start(), calls=%async_computation.26 | async-start | bytes 25067520
  2212.8 494.6 %reduce-scatter.11.cloned.1.call-start = ((), (), s32[]{:S(2)}) async-start(), calls=%async_computation.21 | async-start | bytes 11796480 | tf_op jit(solution)/shard_map/reduce_scatter | solution.py:425
  2225.8 646.7 %reduce-scatter.9.cloned.1.call-start = ((), (), s32[]{:S(2)}) async-start(), calls=%async_computation.20 | async-start | bytes 11796480 | tf_op jit(solution)/shard_map/reduce_scatter | solution.py:425
  2238.4 836.6 %all-reduce.52.cloned.1.call-start = ((), (), s32[]{:S(2)}) async-start(), calls=%async_computation.28 | async-start | bytes 29245440 | tf_op jit(solution)/shard_map/psum | solution.py:430
  (231 other events, 8095.2 us)
Sparse Core Ops, SparseCore 0:
  23.7 400.3 all-gather.22
  425.6 340.9 all-gather.26
  768.7 165.4 all-gather.24
  935.6 164.9 all-gather.28
  1712.4 328.9 reduce-scatter.14
  2212.9 328.9 reduce-scatter.12
  2544.8 162.5 reduce-scatter.10
  2710.3 162.1 reduce-scatter.8
  2876.5 198.4 all-reduce.51
where the time goes:
time: 3120 us; the launch traced here: 3100 us
  waiting for transfers between devices  1310 us (42%)
  local copies, waits for them, and re-layouts  584 us (19%)
  matrix products  435 us (14%)
  other arithmetic  396 us (13%)
  blocking collectives  287 us (9%)
  starting transfers between devices  65.8 us (2%)
    reduce_scatter x2, waiting for transfers between devices, local(): lax.psum_scatter(grad_proj_out.astype(jnp.bfloat16), 'dp', scatter_dimens...  323 us
    unnamed x11, waiting for transfers between devices  268 us
    all_gather x2, waiting for transfers between devices, local(): lax.all_gather(in_weight[layer_index], 'dp', axis=0, tiled=True)  260 us
    unnamed x519, local copies, waits for them, and re-layouts  127 us
    all_gather x2, blocking collectives, local(): lax.all_gather(conv_weight[layer_index], 'dp', axis=1, tiled=True)  124 us
    another operation x16, other arithmetic  116 us
    psum x1, waiting for transfers between devices, local(): lax.psum(grad_parts[0].astype(jnp.bfloat16), 'seq').astype(jnp.float32)  108 us
    all_gather x2, waiting for transfers between devices, local(): lax.all_gather(out_weight[layer_index], 'dp', axis=0, tiled=True)  99.8 us
  transfers between devices with their start and end apart: 25, of which 15 were waited for; matrix products, arithmetic and copies ran while one was open for 36% of the time, Pallas kernels for 0%

commit v1 on v0

v1 whole, which is shorter than its diff:
```python
import functools

import jax
import jax.numpy as jnp
from jax import lax
from jax.experimental import pallas as pl
from jax.experimental.pallas import tpu as pltpu
from jax.sharding import PartitionSpec as P

D = 1536
HEADS = 48
HEAD_DIM = 64
STATE = 128
CONV = 4
BLOCK = 256
LAYERS = 2
DIN = 3072
XBC = DIN + 2 * STATE
REST = XBC + HEADS
PAIRS = HEADS // 2
LANES = 128
HALO = 8

epsilon = 1e-05
highest = lax.Precision.HIGHEST
f32 = jnp.float32
bf16 = jnp.bfloat16
NEG = -1e30


def dot(a, b, ca, cb):
    return lax.dot_general(a, b, (((ca,), (cb,)), ((), ())), preferred_element_type=f32)


def params(semantics, limit=None):
    return pltpu.CompilerParams(dimension_semantics=semantics, vmem_limit_bytes=limit)


def lane_is_low(rows):
    return lax.broadcasted_iota(jnp.int32, (rows, LANES), 1) < HEAD_DIM


def convolve(ext, raw, halo, par):
    rows = raw.shape[0]
    ext[0:HALO, :] = halo.astype(f32)
    ext[HALO : HALO + rows, :] = raw.astype(f32)
    total = par[CONV : CONV + 1, :]
    for tap in range(CONV):
        total = total + par[tap : tap + 1, :] * ext[pl.ds(HALO - CONV + 1 + tap, rows), :]
    return total


def causal_mask():
    i = lax.broadcasted_iota(jnp.int32, (BLOCK, BLOCK), 0)
    j = lax.broadcasted_iota(jnp.int32, (BLOCK, BLOCK), 1)
    return i >= j


def scan_kernel(raw, halo, bc, bc_halo, par, par_bc, rows_ref, direct, states, wbrc, ext, ext_bc, scores):
    pair = pl.program_id(1)

    @pl.when(pair == 0)
    def _():
        conv = convolve(ext_bc, bc[...], bc_halo[...], par_bc)
        act = (conv * jax.nn.sigmoid(conv)).astype(bf16)
        wbrc[...] = act
        scores[...] = dot(act[:, STATE:], act[:, :STATE], 1, 1)

    conv = convolve(ext, raw[...], halo[...], par)
    x = (conv * jax.nn.sigmoid(conv)).astype(bf16).astype(f32)
    rows = rows_ref[0, 0]
    cols = rows.T
    low = lane_is_low(BLOCK)
    mask = causal_mask()
    total = par[CONV + 1 : CONV + 2, :] * x
    for a in range(2):
        mine = low if a == 0 else jnp.logical_not(low)
        x_a = jnp.where(mine, x, 0.0).astype(bf16)
        spread = cols[:, 2 + a : 3 + a] - rows[2 + a : 3 + a, :]
        decay = jnp.exp(jnp.where(mask, spread, NEG))
        mixing = (scores[...] * decay * rows[a : a + 1, :]).astype(bf16)
        total = total + dot(mixing, x_a, 1, 0)
    direct[...] = total
    weight = jnp.where(low, cols[:, 6:7] * cols[:, 0:1], cols[:, 7:8] * cols[:, 1:2])
    states[0, 0] = dot((weight * x).astype(bf16), wbrc[:, :STATE], 0, 0).astype(bf16)


def scan_forward(proj, par, rows):
    seqs = rows.shape[0]
    halo_at = seqs * BLOCK // HALO
    return pl.pallas_call(
        scan_kernel,
        grid=(seqs, PAIRS),
        in_specs=[
            pl.BlockSpec((BLOCK, LANES), lambda s, p: (s, p)),
            pl.BlockSpec((HALO, LANES), lambda s, p: (halo_at + s, p)),
            pl.BlockSpec((BLOCK, 2 * STATE), lambda s, p: (s, DIN // (2 * STATE))),
            pl.BlockSpec((HALO, 2 * STATE), lambda s, p: (halo_at + s, DIN // (2 * STATE))),
            pl.BlockSpec((8, LANES), lambda s, p: (0, p)),
            pl.BlockSpec((8, 2 * STATE), lambda s, p: (0, DIN // (2 * STATE))),
            pl.BlockSpec((1, 1, 8, BLOCK), lambda s, p: (s, p, 0, 0)),
        ],
        out_specs=[
            pl.BlockSpec((BLOCK, LANES), lambda s, p: (s, p)),
            pl.BlockSpec((1, 1, LANES, STATE), lambda s, p: (s, p, 0, 0)),
            pl.BlockSpec((BLOCK, 2 * STATE), lambda s, p: (s, 0)),
        ],
        out_shape=[
            jax.ShapeDtypeStruct((seqs * BLOCK, DIN), f32),
            jax.ShapeDtypeStruct((seqs, PAIRS, LANES, STATE), bf16),
            jax.ShapeDtypeStruct((seqs * BLOCK, 2 * STATE), bf16),
        ],
        scratch_shapes=[
            pltpu.VMEM((BLOCK + HALO, LANES), f32),
            pltpu.VMEM((BLOCK + HALO, 2 * STATE), f32),
            pltpu.VMEM((BLOCK, BLOCK), f32),
        ],
        compiler_params=params(("arbitrary", "arbitrary")),
        cost_estimate=pl.CostEstimate(
            flops=seqs * PAIRS * 4 * BLOCK * BLOCK * LANES,
            bytes_accessed=seqs * BLOCK * DIN * 6,
            transcendentals=seqs * HEADS * BLOCK * BLOCK,
        ),
        name="scan_forward",
    )(proj, proj, proj, proj, par, par, rows)


def gate_kernel(direct, gate, rc, rows_ref, entering, gain, y_ref, out, kept):
    tile = direct.shape[0]
    low = lane_is_low(tile)

    def body(pair, squares):
        at = pl.ds(pl.multiple_of(pair * LANES, LANES), LANES)
        cols = rows_ref[0, pair].T
        readout = dot(rc[...], entering[0, pair], 1, 1)
        y = (direct[:, at] + jnp.where(low, cols[:, 4:5], cols[:, 5:6]) * readout).astype(bf16)
        y_ref[:, at] = y
        g = gate[:, at].astype(f32)
        gated = y.astype(f32) * (g * jax.nn.sigmoid(g))
        kept[:, at] = gated
        return squares + gated * gated

    squares = lax.fori_loop(0, PAIRS, body, jnp.zeros((tile, LANES), f32))
    scale = lax.rsqrt(jnp.sum(squares, -1, keepdims=True) * (1.0 / DIN) + epsilon)
    out[...] = (kept[...] * scale * gain[...]).astype(bf16)


def gate_forward(direct, gate, wbrc, rows, entering, gain):
    seqs = rows.shape[0]
    tile = 128
    parts = BLOCK // tile
    wide = pl.BlockSpec((tile, DIN), lambda s, r: (s * parts + r, 0))
    return pl.pallas_call(
        gate_kernel,
        grid=(seqs, parts),
        in_specs=[
            wide,
            wide,
            pl.BlockSpec((tile, STATE), lambda s, r: (s * parts + r, 1)),
            pl.BlockSpec((1, PAIRS, 8, tile), lambda s, r: (s, 0, 0, r)),
            pl.BlockSpec((1, PAIRS, LANES, STATE), lambda s, r: (s, 0, 0, 0)),
            pl.BlockSpec((1, DIN), lambda s, r: (0, 0)),
        ],
        out_specs=[wide, wide],
        out_shape=[
            jax.ShapeDtypeStruct((seqs * BLOCK, DIN), bf16),
            jax.ShapeDtypeStruct((seqs * BLOCK, DIN), bf16),
        ],
        scratch_shapes=[pltpu.VMEM((tile, DIN), f32)],
        compiler_params=params(("arbitrary", "arbitrary")),
        cost_estimate=pl.CostEstimate(
            flops=2 * seqs * BLOCK * DIN * STATE,
            bytes_accessed=seqs * BLOCK * DIN * 10,
            transcendentals=seqs * BLOCK * DIN,
        ),
        name="gate_forward",
    )(direct, gate, wbrc, rows, entering, gain)


def gate_back_kernel(grad, y_ref, gate, gain, rc, rows_ref, g_y, g_gate, g_entering, g_gain):
    low = lane_is_low(BLOCK)

    def at_pair(pair):
        return pl.ds(pl.multiple_of(pair * LANES, LANES), LANES)

    def parts(pair):
        at = at_pair(pair)
        g = gate[:, at].astype(f32)
        sig = jax.nn.sigmoid(g)
        y = y_ref[:, at].astype(f32)
        return at, g, sig, y, y * (g * sig)

    def first(pair, sums):
        at, _, _, _, gated = parts(pair)
        return sums[0] + gated * gated, sums[1] + grad[:, at] * gain[:, at] * gated

    zero = jnp.zeros((BLOCK, LANES), f32)
    squares, products = lax.fori_loop(0, PAIRS, first, (zero, zero))
    scale = lax.rsqrt(jnp.sum(squares, -1, keepdims=True) * (1.0 / DIN) + epsilon)
    back = scale * scale * scale * (jnp.sum(products, -1, keepdims=True) * (1.0 / DIN))

    @pl.when(pl.program_id(0) == 0)
    def _():
        g_gain[...] = jnp.zeros_like(g_gain)

    def second(pair, carry):
        at, g, sig, y, gated = parts(pair)
        incoming = grad[:, at]
        g_gain[:, at] += jnp.sum((incoming * gated * scale).reshape(BLOCK // 8, 8, LANES), 0)
        g_gated = scale * incoming * gain[:, at] - gated * back
        grad_y = (g_gated * (g * sig)).astype(bf16)
        g_y[:, at] = grad_y
        g_gate[:, at] = (g_gated * y * (sig * (1.0 + g * (1.0 - sig)))).astype(bf16)
        cols = rows_ref[0, pair].T
        g_read = (jnp.where(low, cols[:, 4:5], cols[:, 5:6]) * grad_y.astype(f32)).astype(bf16)
        g_entering[0, pair] = dot(g_read, rc[...], 0, 0).astype(bf16)
        return carry

    lax.fori_loop(0, PAIRS, second, 0)


def gate_backward(grad, y, gate, gain, wbrc, rows):
    seqs = rows.shape[0]
    wide = pl.BlockSpec((BLOCK, DIN), lambda s: (s, 0))
    return pl.pallas_call(
        gate_back_kernel,
        grid=(seqs,),
        in_specs=[
            wide,
            wide,
            wide,
            pl.BlockSpec((1, DIN), lambda s: (0, 0)),
            pl.BlockSpec((BLOCK, STATE), lambda s: (s, 1)),
            pl.BlockSpec((1, PAIRS, 8, BLOCK), lambda s: (s, 0, 0, 0)),
        ],
        out_specs=[
            wide,
            wide,
            pl.BlockSpec((1, PAIRS, LANES, STATE), lambda s: (s, 0, 0, 0)),
            pl.BlockSpec((8, DIN), lambda s: (0, 0)),
        ],
        out_shape=[
            jax.ShapeDtypeStruct((seqs * BLOCK, DIN), bf16),
            jax.ShapeDtypeStruct((seqs * BLOCK, DIN), bf16),
            jax.ShapeDtypeStruct((seqs, PAIRS, LANES, STATE), bf16),
            jax.ShapeDtypeStruct((8, DIN), f32),
        ],
        compiler_params=params(("arbitrary",)),
        cost_estimate=pl.CostEstimate(
            flops=2 * seqs * BLOCK * DIN * STATE,
            bytes_accessed=seqs * BLOCK * DIN * 12,
            transcendentals=2 * seqs * BLOCK * DIN,
        ),
        name="gate_backward",
    )(grad, y, gate, gain, wbrc, rows)


def scan_back_kernel(
    raw, halo, grad, par, rows_ref, wbrc, entering, g_states,
    g_raw, g_halo, g_par, g_rows,
    ext, gext, g_act, scores, g_scores, g_wb, g_rc,
):
    step = pl.program_id(1)

    @pl.when(step == 0)
    def _():
        scores[...] = dot(wbrc[:, STATE:], wbrc[:, :STATE], 1, 1)
        g_scores[...] = jnp.zeros_like(g_scores)
        g_wb[...] = jnp.zeros_like(g_wb)
        g_rc[...] = jnp.zeros_like(g_rc)

    conv = convolve(ext, raw[...], halo[...], par)
    sig = jax.nn.sigmoid(conv)
    g_par[...] = jnp.zeros_like(g_par)

    @pl.when(step < PAIRS)
    def _():
        x = (conv * sig).astype(bf16).astype(f32)
        gy = grad[...].astype(f32)
        rows = rows_ref[0, 0]
        cols = rows.T
        low = lane_is_low(BLOCK)
        mask = causal_mask()
        wb = wbrc[:, :STATE]
        rc = wbrc[:, STATE:]
        ent = entering[0, 0]
        g_st = g_states[0, 0]

        def head_sums(values):
            first = jnp.sum(jnp.where(low, values, 0.0), -1, keepdims=True)
            second = jnp.sum(jnp.where(low, 0.0, values), -1, keepdims=True)
            return first, second

        e_cum = jnp.where(low, cols[:, 4:5], cols[:, 5:6])
        weight = jnp.where(low, cols[:, 6:7] * cols[:, 0:1], cols[:, 7:8] * cols[:, 1:2])
        readout = dot(rc, ent, 1, 1)
        g_read = e_cum * gy
        read_sums = head_sums(g_read * readout)
        g_rc[...] += dot(g_read.astype(bf16), ent, 1, 0)
        spread_back = dot(wb, g_st, 1, 1)
        weight_sums = head_sums(x * spread_back)
        g_wb[...] += dot((weight * x).astype(bf16), g_st, 1, 0)
        g_x = par[CONV + 1 : CONV + 2, :] * gy + weight * spread_back
        state_products = g_st.astype(f32) * ent.astype(f32)
        last = lax.broadcasted_iota(jnp.int32, (BLOCK, 1), 0) == BLOCK - 1
        lane = lax.broadcasted_iota(jnp.int32, (BLOCK, LANES), 1)
        columns = jnp.zeros((BLOCK, LANES), f32)
        row_parts = []
        for a in range(2):
            mine = low if a == 0 else jnp.logical_not(low)
            x_a = jnp.where(mine, x, 0.0).astype(bf16)
            gy_a = jnp.where(mine, gy, 0.0).astype(bf16)
            dt_row = rows[a : a + 1, :]
            g_mixing = dot(gy_a, x_a, 1, 1)
            spread = cols[:, 2 + a : 3 + a] - rows[2 + a : 3 + a, :]
            decay = jnp.exp(jnp.where(mask, spread, NEG))
            s = scores[...]
            mixing = (s * decay * dt_row).astype(bf16)
            g_x = g_x + dot(mixing, gy_a, 0, 0)
            t = g_mixing * decay
            g_scores[...] += t * dt_row
            q = t * s
            row_sum = jnp.sum(q * dt_row, -1, keepdims=True)
            col_sum = jnp.sum(q, 0, keepdims=True)
            w_col = cols[:, 6 + a : 7 + a] * cols[:, a : a + 1]
            weighted = weight_sums[a] * w_col
            e_total = jnp.exp(rows[2 + a : 3 + a, BLOCK - 1 :])
            pieces = state_products[a * HEAD_DIM : (a + 1) * HEAD_DIM, :]
            g_total = e_total * jnp.sum(jnp.sum(pieces, 0, keepdims=True), 1, keepdims=True)
            g_total = g_total + jnp.sum(weighted, 0, keepdims=True)
            g_cum = row_sum + read_sums[a] - weighted + jnp.where(last, g_total, 0.0)
            g_dt = weight_sums[a] * cols[:, 6 + a : 7 + a]
            columns = jnp.where(lane == a, g_cum, columns)
            columns = jnp.where(lane == 2 + a, g_dt, columns)
            row_parts.append((-dt_row * col_sum, col_sum))
        turned = columns.T[0:8, :]
        row = lax.broadcasted_iota(jnp.int32, (8, BLOCK), 0)
        for a in range(2):
            turned = turned + jnp.where(row == a, row_parts[a][0], 0.0)
            turned = turned + jnp.where(row == 2 + a, row_parts[a][1], 0.0)
        g_rows[0, 0] = turned
        g_act[...] = g_x
        g_par[CONV + 1 : CONV + 2, :] = jnp.sum(gy * x, 0, keepdims=True)

    @pl.when(step == PAIRS)
    def _():
        g_s = g_scores[...]
        g_high = g_s.astype(bf16)
        g_low = (g_s - g_high.astype(f32)).astype(bf16)
        wb = wbrc[:, :STATE]
        rc = wbrc[:, STATE:]
        g_act[...] = g_wb[...] + dot(g_high, rc, 0, 0) + dot(g_low, rc, 0, 0)
        g_rc[...] = g_rc[...] + dot(g_high, wb, 1, 0) + dot(g_low, wb, 1, 0)

    @pl.when(step == PAIRS + 1)
    def _():
        g_act[...] = g_rc[...]

    g_conv = g_act[...] * (sig * (1.0 + conv * (1.0 - sig)))
    gext[0:HALO, :] = jnp.zeros((HALO, LANES), f32)
    gext[HALO : HALO + BLOCK, :] = g_conv
    gext[HALO + BLOCK :, :] = jnp.zeros((HALO, LANES), f32)
    inside = jnp.zeros((BLOCK, LANES), f32)
    before = jnp.zeros((HALO, LANES), f32)
    for tap in range(CONV):
        ahead = CONV - 1 - tap
        factor = par[tap : tap + 1, :]
        inside = inside + factor * gext[pl.ds(HALO + ahead, BLOCK), :]
        before = before + factor * gext[pl.ds(ahead, HALO), :]
        g_par[tap : tap + 1, :] = jnp.sum(
            g_conv * ext[pl.ds(HALO - CONV + 1 + tap, BLOCK), :], 0, keepdims=True
        )
    g_par[CONV : CONV + 1, :] = jnp.sum(g_conv, 0, keepdims=True)
    g_raw[...] = inside.astype(bf16)
    g_halo[...] = before


def scan_backward(proj, grad, par, rows, wbrc, entering, g_states):
    seqs = rows.shape[0]
    halo_at = seqs * BLOCK // HALO

    def clip(p):
        return jnp.minimum(p, PAIRS - 1)

    small = pl.BlockSpec((1, 1, LANES, STATE), lambda s, p: (s, clip(p), 0, 0))
    return pl.pallas_call(
        scan_back_kernel,
        grid=(seqs, PAIRS + 2),
        in_specs=[
            pl.BlockSpec((BLOCK, LANES), lambda s, p: (s, p)),
            pl.BlockSpec((HALO, LANES), lambda s, p: (halo_at + s, p)),
            pl.BlockSpec((BLOCK, LANES), lambda s, p: (s, clip(p))),
            pl.BlockSpec((8, LANES), lambda s, p: (0, p)),
            pl.BlockSpec((1, 1, 8, BLOCK), lambda s, p: (s, clip(p), 0, 0)),
            pl.BlockSpec((BLOCK, 2 * STATE), lambda s, p: (s, 0)),
            small,
            small,
        ],
        out_specs=[
            pl.BlockSpec((BLOCK, LANES), lambda s, p: (s, p)),
            pl.BlockSpec((HALO, LANES), lambda s, p: (s, p)),
            pl.BlockSpec((8, LANES), lambda s, p: (s, p)),
            pl.BlockSpec((1, 1, 8, BLOCK), lambda s, p: (s, clip(p), 0, 0)),
        ],
        out_shape=[
            jax.ShapeDtypeStruct((seqs * BLOCK, REST), bf16),
            jax.ShapeDtypeStruct((seqs * HALO, XBC), f32),
            jax.ShapeDtypeStruct((seqs * 8, XBC), f32),
            jax.ShapeDtypeStruct((seqs, PAIRS, 8, BLOCK), f32),
        ],
        scratch_shapes=[
            pltpu.VMEM((BLOCK + HALO, LANES), f32),
            pltpu.VMEM((BLOCK + 2 * HALO, LANES), f32),
            pltpu.VMEM((BLOCK, LANES), f32),
            pltpu.VMEM((BLOCK, BLOCK), f32),
            pltpu.VMEM((BLOCK, BLOCK), f32),
            pltpu.VMEM((BLOCK, STATE), f32),
            pltpu.VMEM((BLOCK, STATE), f32),
        ],
        compiler_params=params(("arbitrary", "arbitrary")),
        cost_estimate=pl.CostEstimate(
            flops=seqs * PAIRS * 10 * BLOCK * BLOCK * LANES,
            bytes_accessed=seqs * BLOCK * DIN * 6,
            transcendentals=seqs * HEADS * BLOCK * BLOCK,
        ),
        name="scan_backward",
    )(proj, proj, grad, par, rows, wbrc, entering, g_states)


def gather_weight(shard, seq_total, seq_rank):
    piece = shard.shape[0] // seq_total
    mine = lax.dynamic_slice_in_dim(shard, seq_rank * piece, piece, 0)
    return lax.all_gather(mine, ("dp", "seq"), axis=0, tiled=True)


def reduce_weight(grad):
    mine = lax.psum_scatter(grad, ("dp", "seq"), scatter_dimension=0, tiled=True)
    return lax.all_gather(mine, "seq", axis=0, tiled=True)


def shift(values, total, by):
    if by > 0:
        pairs = [(i, i + 1) for i in range(total - 1)]
    else:
        pairs = [(i + 1, i) for i in range(total - 1)]
    return lax.ppermute(values, "seq", pairs)


def exchange(values):
    return lax.all_to_all(values, "seq", split_axis=0, concat_axis=0, tiled=True)


def carry_states(states, decays, seq_total, forward):
    shape = states.shape
    items = shape[0] // seq_total
    blocks = states.reshape((seq_total, items) + shape[1:])
    running = jnp.zeros(blocks.shape[1:], f32)
    found = [None] * seq_total
    for at in range(seq_total) if forward else reversed(range(seq_total)):
        found[at] = running.astype(bf16)
        running = decays[at][:, None, None] * running + blocks[at].astype(f32)
    return jnp.stack(found, 0).reshape(shape)


def local(
    hidden, lengths, cotangent, norm_gain, in_weight, conv_weight, conv_bias,
    dt_bias, decay_log, skip_gain, gate_gain, out_weight,
):
    seq_total = lax.axis_size("seq")
    seq_rank = lax.axis_index("seq")
    data_total = lax.axis_size("dp")
    data_rank = lax.axis_index("dp")
    seqs = hidden.shape[0]
    tokens = seqs * BLOCK
    items = seqs * HEADS // seq_total
    positions = seq_rank * BLOCK + jnp.arange(BLOCK)
    valid = (positions[None, :] < lengths[:, None]).astype(f32).reshape(tokens, 1)

    small = lax.all_gather(
        jnp.concatenate(
            [
                norm_gain,
                conv_weight.reshape(LAYERS, -1),
                conv_bias,
                dt_bias,
                decay_log,
                skip_gain,
                gate_gain,
            ],
            1,
        ),
        "dp",
        axis=0,
    ).astype(f32)
    widths = [D, CONV * XBC, XBC, HEADS, HEADS, HEADS, DIN]
    split_at = []
    running = 0
    for width in widths:
        split_at.append((running, width // data_total))
        running += width // data_total

    def small_of(member, layer):
        start, size = split_at[member]
        values = small[:, layer, start : start + size]
        if member == 1:
            taps = values.reshape(data_total, CONV, XBC // data_total)
            return taps.transpose(1, 0, 2).reshape(CONV, XBC)
        return values.reshape(-1)

    weights = []
    for layer in range(LAYERS):
        weights.append(
            (
                gather_weight(in_weight[layer, :, DIN:], seq_total, seq_rank),
                gather_weight(in_weight[layer, :, :DIN], seq_total, seq_rank),
                gather_weight(out_weight[layer], seq_total, seq_rank),
            )
        )

    lower = (jnp.arange(BLOCK)[:, None] >= jnp.arange(BLOCK)[None, :]).astype(f32)
    h = hidden.astype(f32).reshape(tokens, D)
    kept = []
    squares = []
    for layer in range(LAYERS):
        gain = small_of(0, layer)
        taps, bias = small_of(1, layer), small_of(2, layer)
        step_bias, log_rate = small_of(3, layer), small_of(4, layer)
        skip, gated_gain = small_of(5, layer), small_of(6, layer)[None]
        w_rest, w_gate, w_out = weights[layer]
        par = jnp.concatenate(
            [
                taps,
                bias[None],
                jnp.concatenate([jnp.repeat(skip, HEAD_DIM), jnp.zeros((2 * STATE,), f32)])[None],
                jnp.zeros((2, XBC), f32),
            ],
            0,
        )
        halo = shift(h.reshape(seqs, BLOCK, D)[:, BLOCK - HALO :], seq_total, 1)
        h_more = jnp.concatenate([h, halo.reshape(seqs * HALO, D)], 0)
        scale = lax.rsqrt(jnp.mean(h_more * h_more, -1, keepdims=True) + epsilon)
        normed_more = (h_more * scale * gain).astype(bf16)
        normed = normed_more[:tokens]
        proj = dot(normed_more, w_rest, 1, 0).astype(bf16)
        gate = dot(normed, w_gate, 1, 0).astype(bf16)
        step_in = proj[:tokens, XBC:].reshape(seqs, BLOCK, HEADS).astype(f32).transpose(0, 2, 1)
        step_in = step_in + step_bias[:, None]
        dt = jax.nn.softplus(step_in)
        speed = jnp.exp(log_rate)[:, None]
        cum = jnp.einsum("shj,ij->shi", -dt * speed, lower, precision=highest)
        total = cum[..., -1]
        rows = jnp.stack([dt, cum, jnp.exp(cum), jnp.exp(total[..., None] - cum)], 2)
        rows = rows.reshape(seqs, PAIRS, 2, 4, BLOCK).transpose(0, 1, 3, 2, 4)
        rows = rows.reshape(seqs, PAIRS, 8, BLOCK)
        totals = lax.all_gather(total.reshape(-1), "seq", axis=0)
        decays = jnp.exp(lax.dynamic_slice_in_dim(totals, seq_rank * items, items, 1))
        direct, states, wbrc = scan_forward(proj, par, rows)
        entering = exchange(
            carry_states(
                exchange(states.reshape(seqs * HEADS, HEAD_DIM, STATE)), decays, seq_total, True
            )
        ).reshape(states.shape)
        y, gated = gate_forward(direct, gate, wbrc, rows, entering, gated_gain)
        mixer = dot(gated, w_out, 1, 0)
        squares.append(jnp.sum(h * h * valid))
        squares.append(jnp.sum(mixer * mixer * valid))
        kept.append(
            (h, scale[:tokens], gain, normed, proj, gate, step_in, dt, speed, par, rows, decays,
             wbrc, entering, y, gated, gated_gain)
        )
        h = h + mixer
    output = (h * valid).reshape(hidden.shape)

    g = cotangent.astype(f32).reshape(tokens, D) * valid
    large_in = [None] * LAYERS
    large_out = [None] * LAYERS
    sums = [None] * LAYERS
    for layer in reversed(range(LAYERS)):
        (h_in, scale, gain, normed, proj, gate, step_in, dt, speed, par, rows, decays,
         wbrc, entering, y, gated, gated_gain) = kept[layer]
        w_rest, w_gate, w_out = weights[layer]
        g_low = g.astype(bf16)
        grad_out = reduce_weight(dot(gated, g_low, 0, 0).astype(bf16))
        g_gated = dot(g_low, w_out, 1, 1)
        g_y, g_gate, g_entering, g_gated_gain = gate_backward(
            g_gated, y, gate, gated_gain, wbrc, rows
        )
        grad_gate = reduce_weight(dot(normed, g_gate, 0, 0).astype(bf16))
        g_states = exchange(
            carry_states(
                exchange(g_entering.reshape(seqs * HEADS, HEAD_DIM, STATE)),
                decays,
                seq_total,
                False,
            )
        ).reshape(g_entering.shape)
        g_raw, g_halo, g_par, g_rows = scan_backward(
            proj, g_y, par, rows, wbrc, entering, g_states
        )
        g_rows = g_rows[:, :, :4].reshape(seqs, PAIRS, 2, 2, BLOCK).transpose(2, 0, 1, 3, 4)
        g_rows = g_rows.reshape(2, seqs, HEADS, BLOCK)
        g_rate = jnp.einsum("shi,ij->shj", g_rows[0], lower, precision=highest)
        g_dt = g_rows[1] - speed * g_rate
        g_step = g_dt * jax.nn.sigmoid(step_in)
        g_log = jnp.sum(-dt * speed * g_rate, (0, 2))
        from_next = shift(g_halo.reshape(seqs, HALO, XBC), seq_total, -1)
        tail = g_raw.reshape(seqs, BLOCK, REST)[:, BLOCK - HALO :, :XBC].astype(f32) + from_next
        g_rest = g_raw.reshape(seqs, BLOCK, REST)
        g_rest = lax.dynamic_update_slice(g_rest, tail.astype(bf16), (0, BLOCK - HALO, 0))
        g_rest = lax.dynamic_update_slice(
            g_rest, g_step.transpose(0, 2, 1).astype(bf16), (0, 0, XBC)
        ).reshape(tokens, REST)
        grad_rest = reduce_weight(dot(normed, g_rest, 0, 0).astype(bf16))
        g_normed = dot(g_gate, w_gate, 1, 1) + dot(g_rest, w_rest, 1, 1)
        scaled = g_normed * gain
        inner = jnp.mean(scaled * h_in, -1, keepdims=True)
        g = g + scale * scaled - h_in * (scale * scale * scale * inner)
        g_gain = jnp.sum(g_normed * h_in * scale, 0)
        g_par = jnp.sum(g_par.reshape(seqs, 8, XBC), 0)
        sums[layer] = (
            g_gain,
            g_par[:CONV].reshape(-1),
            g_par[CONV],
            jnp.sum(g_step, (0, 2)),
            g_log,
            jnp.sum(g_par[CONV + 1, :DIN].reshape(HEADS, HEAD_DIM), 1),
            jnp.sum(g_gated_gain, 0),
        )
        large_in[layer] = jnp.concatenate([grad_gate, grad_rest], 1).astype(f32)
        large_out[layer] = grad_out.astype(f32)

    flat = jnp.concatenate(
        [part for layer_sums in sums for part in layer_sums]
        + [jnp.stack(squares), jnp.sum(valid)[None]]
    )
    flat = lax.psum(flat, ("dp", "seq"))
    norm_stats = jnp.sqrt(flat[-5:-1].reshape(LAYERS, 2) / (flat[-1] * D))
    whole = flat[:-5].reshape(LAYERS, -1)
    found = []
    start = 0
    for member, width in enumerate(widths):
        values = whole[:, start : start + width]
        start += width
        piece = width // data_total
        if member == 1:
            values = values.reshape(LAYERS, CONV, XBC)
            piece = XBC // data_total
        found.append(
            lax.dynamic_slice_in_dim(values, data_rank * piece, piece, values.ndim - 1)
        )
    return (
        output,
        g.reshape(hidden.shape),
        found[0],
        jnp.stack(large_in, 0),
        found[1],
        found[2],
        found[3],
        found[4],
        found[5],
        found[6],
        jnp.stack(large_out, 0),
        norm_stats,
    )


def solution(mesh):
    return jax.shard_map(
        local,
        mesh=mesh,
        in_specs=(
            P("dp", "seq", None),
            P("dp"),
            P("dp", "seq", None),
            P(None, "dp"),
            P(None, "dp", None),
            P(None, None, "dp"),
            P(None, "dp"),
            P(None, "dp"),
            P(None, "dp"),
            P(None, "dp"),
            P(None, "dp"),
            P(None, "dp", None),
        ),
        out_specs=(
            P("dp", "seq", None),
            P("dp", "seq", None),
            P(None, "dp"),
            P(None, "dp", None),
            P(None, None, "dp"),
            P(None, "dp"),
            P(None, "dp"),
            P(None, "dp"),
            P(None, "dp"),
            P(None, "dp"),
            P(None, "dp", None),
            P(),
        ),
        check_vma=False,
    )
```

time: 3120 us -> 1940 us (0.62)
  local copies, waits for them, and re-layouts: 584 us -> 113 us
  Pallas kernels: 0 us -> 398 us
  waiting for transfers between devices: 1310 us -> 980 us
  other arithmetic: 396 us -> 73.7 us
  matrix products: 435 us -> 183 us
  blocking collectives: 287 us -> 124 us
  starting transfers between devices: 65.8 us -> 33.1 us
    pallas_call x0 -> x8, Pallas kernels: none -> 398 us  [the longest x2 186 us: scan_backward(): pl.pallas_call(scan_back_kernel, grid=(seqs, PAIRS + 2), in_specs=[pl.Blo...]
    unnamed x11 -> x19, waiting for transfers between devices: 268 us -> 1.28 us
    dot_general x48 -> x22, matrix products: 435 us -> 183 us  [the longest x18 180 us: dot(): lax.dot_general(a, b, (((ca,), (cb,)), ((), ())), preferred_element_type=...]
    all_to_all x16 -> x6, waiting for transfers between devices: 253 us -> 44.8 us  [exchange(): lax.all_to_all(values, 'seq', split_axis=0, concat_axis=0, tiled=True)]
    convert_element_type x24 -> x4, local copies, waits for them, and re-layouts: 167 us -> 0.42 us  [the longest x2 0.24 us: local(): g_step.transpose(0, 2, 1).astype(bf16)]
    reshape x34 -> x13, local copies, waits for them, and re-layouts: 163 us -> 8.97 us  [the longest x2 2.8 us: local(): jnp.repeat(skip, HEAD_DIM)]
    all_gather x6 -> x3, blocking collectives: 195 us -> 67.1 us  [the longest x2 52.5 us: local(): totals = lax.all_gather(total.reshape(-1), 'seq', axis=0)]
    another operation x30 -> x4, other arithmetic: 142 us -> 20.3 us  [the longest x1 10.9 us: local(): jnp.stack(large_in, 0)]
  transfers between devices with their start and end apart: 25 -> 29, of which waited for: 15 -> 20; matrix products, arithmetic and copies ran while one was open for 36% -> 16% of each run, Pallas kernels for 0% -> 17%
where the time goes in v1:
time: 1940 us; the launch traced here: 1920 us
  waiting for transfers between devices  980 us (51%)
  Pallas kernels  398 us (21%)
  matrix products  183 us (9%)
  blocking collectives  124 us (6%)
  local copies, waits for them, and re-layouts  113 us (6%)
  other arithmetic  73.7 us (4%)
  starting transfers between devices  33.1 us (2%)
    reduce_scatter x6, waiting for transfers between devices, reduce_weight(): lax.psum_scatter(grad, ('dp', 'seq'), scatter_dimension=0, tiled=True)  444 us
    all_gather x6, waiting for transfers between devices, gather_weight(): return lax.all_gather(mine, ('dp', 'seq'), axis=0, tiled=True)  193 us
    pallas_call x2, Pallas kernels, scan_backward(): pl.pallas_call(scan_back_kernel, grid=(seqs, PAIRS + 2), in_specs=[pl.Blo...  186 us
    dot_general x18, matrix products, dot(): lax.dot_general(a, b, (((ca,), (cb,)), ((), ())), preferred_element_type=...  180 us
    all_gather x6, waiting for transfers between devices, reduce_weight(): return lax.all_gather(mine, 'seq', axis=0, tiled=True)  173 us
    psum x1, waiting for transfers between devices, local(): flat = lax.psum(flat, ('dp', 'seq'))  121 us
    pallas_call x2, Pallas kernels, scan_forward(): pl.pallas_call(scan_kernel, grid=(seqs, PAIRS), in_specs=[pl.BlockSpec((B...  80.9 us
    pallas_call x2, Pallas kernels, gate_backward(): pl.pallas_call(gate_back_kernel, grid=(seqs,), in_specs=[wide, wide, wide...  73.8 us
  transfers between devices with their start and end apart: 29, of which 20 were waited for; matrix products, arithmetic and copies ran while one was open for 16% of the time, Pallas kernels for 17%

profile of v1, /device:TPU:0, one launch (start us, length us, event | category | flops | bytes accessed | tf_op | source)
XLA Modules:
  0.0 1921.1 jit_solution(13672341361433176098)
XLA Ops:
  118.9 40.4 %scan_forward.2 = (f32[512,3072]{1,0:T(8,128)}, bf16[2,24,128,128]{3,2,1,0:T(8,128)(2,1)}, bf16[512,256]{1,0:T(8,128)(2,1)}) custom-call(bf16[528,3376]{1,0:T(8,128)(2,1)} %copy-done, bf16[528,3376]{1,0:T(8,128)(2,1)} %copy-done, bf16[528,3376]{1,0:T(8,128)(2,1)} %copy-done, bf16[528,3376]{1,0:T(8,128)(2,1)} %copy-done, ...), custom_call_target="tpu_custom_call" | custom-call | flops 1610612736 | bytes 9437184 | tf_op jit(solution)/shard_map/scan_forward/pallas_call | solution.py:91
  163.8 31.0 %all-gather.8 = f32[8,1,96]{2,1,0:T(1,128)S(1)} all-gather(f32[1,1,96]{2,1,0:T(1,128)S(1)} %reshape.723), channel_id=1, replica_groups=mesh['dp'=4,'seq'=8] {'seq'}, dimensions={0}, use_global_device_ids=true | all-gather | bytes 3456 | tf_op jit(solution)/shard_map/all_gather | solution.py:555
  229.5 28.5 %gate_forward.2 = (bf16[512,3072]{1,0:T(8,128)(2,1)}, bf16[512,3072]{1,0:T(8,128)(2,1)}) custom-call(f32[512,3072]{1,0:T(8,128)} %get-tuple-element.38.direct, bf16[512,3072]{1,0:T(8,128)(2,1)} %fusion.30.gate, bf16[512,256]{1,0:T(8,128)(2,1)} %get-tuple-element.39.rc.wbrc, f32[2,24,8,256]{3,2,1,0:T(8,128)} %reshape.672.rows_ref, ...), custom_call_target="tpu_custom_call" | custom-call | flops 402653184 | bytes 15728640 | tf_op jit(solution)/shard_map/gate_forward/pallas_call | solution.py:153
  258.0 34.9 %all-gather.39.cloned.1.call-done = bf16[1,3072,1536]{2,1,0:T(8,128)(2,1)} async-done(((bf16[1,96,1536]{2,1,0:T(8,128)(2,1)}), bf16[1,3072,1536]{2,1,0:T(8,128)(2,1)}) %all-gather.39.cloned.1.call-update) | async-done | bytes 9437200 | tf_op jit(solution)/shard_map/all_gather | solution.py:433
  308.8 72.5 %all-gather.41.cloned.1.call-done = bf16[1,1536,3376]{2,1,0:T(8,128)(2,1)} async-done(((bf16[1,48,3376]{2,1,0:T(8,128)(2,1)}), bf16[1,1536,3376]{2,1,0:T(8,128)(2,1)}) %all-gather.41.cloned.1.call-update) | async-done | bytes 10371088 | tf_op jit(solution)/shard_map/all_gather | solution.py:433
  401.0 40.4 %scan_forward.3 = (f32[512,3072]{1,0:T(8,128)}, bf16[2,24,128,128]{3,2,1,0:T(8,128)(2,1)}, bf16[512,256]{1,0:T(8,128)(2,1)}) custom-call(bf16[528,3376]{1,0:T(8,128)(2,1)} %copy-done.1, bf16[528,3376]{1,0:T(8,128)(2,1)} %copy-done.1, bf16[528,3376]{1,0:T(8,128)(2,1)} %copy-done.1, bf16[528,3376]{1,0:T(8,128)(2,1)} %copy-done.1, ...), custom_call_target="tpu_custom_call" | custom-call | flops 1610612736 | bytes 9437184 | tf_op jit(solution)/shard_map/scan_forward/pallas_call | solution.py:91
  499.7 63.4 %all-gather.43.cloned.1.call-done = bf16[1,1536,3072]{2,1,0:T(8,128)(2,1)} async-done(((bf16[1,48,3072]{2,1,0:T(8,128)(2,1)}), bf16[1,1536,3072]{2,1,0:T(8,128)(2,1)}) %all-gather.43.cloned.1.call-update) | async-done | bytes 9437200 | tf_op jit(solution)/shard_map/all_gather | solution.py:433
  572.3 28.5 %gate_forward.3 = (bf16[512,3072]{1,0:T(8,128)(2,1)}, bf16[512,3072]{1,0:T(8,128)(2,1)}) custom-call(f32[512,3072]{1,0:T(8,128)} %get-tuple-element.42.direct, bf16[512,3072]{1,0:T(8,128)(2,1)} %fusion.33.gate, bf16[512,256]{1,0:T(8,128)(2,1)} %get-tuple-element.43.rc.wbrc, f32[2,24,8,256]{3,2,1,0:T(8,128)} %reshape.680.rows_ref, ...), custom_call_target="tpu_custom_call" | custom-call | flops 402653184 | bytes 15728640 | tf_op jit(solution)/shard_map/gate_forward/pallas_call | solution.py:153
  600.8 36.5 %gate_backward.2 = (bf16[512,3072]{1,0:T(8,128)(2,1)}, bf16[512,3072]{1,0:T(8,128)(2,1)}, bf16[2,24,128,128]{3,2,1,0:T(8,128)(2,1)}, f32[8,3072]{1,0:T(8,128)}) custom-call(f32[512,3072]{1,0:T(8,128)} %fusion.8.grad, bf16[512,3072]{1,0:T(8,128)(2,1)} %get-tuple-element.46.y_ref, bf16[512,3072]{1,0:T(8,128)(2,1)} %fusion.33.gate, f32[1,3072]{1,0:T(1,128)} %bitcast.407, ...), custom_call_target="tpu_custom_call" | custom-call | flops 402653184 | bytes 18874368 | tf_op jit(solution)/shard_map/gate_backward/pallas_call | solution.py:225
  697.6 93.0 %scan_backward.2 = (bf16[512,3376]{1,0:T(8,128)(2,1)}, f32[16,3328]{1,0:T(8,128)}, f32[16,3328]{1,0:T(8,128)}, f32[2,24,8,256]{3,2,1,0:T(8,128)}) custom-call(bf16[528,3376]{1,0:T(8,128)(2,1)} %copy-done.1, bf16[528,3376]{1,0:T(8,128)(2,1)} %copy-done.1, bf16[512,3072]{1,0:T(8,128)(2,1)} %get-tuple-element.48.grad, f32[8,3328]{1,0:T(8,128)} %get-tuple-element.186.par.par_bc, ...), custom_call_target="tpu_custom_call" | custom-call | flops 4026531840 | bytes 9437184 | tf_op jit(solution)/shard_map/scan_backward/pallas_call | solution.py:386
  864.1 37.2 %gate_backward.3 = (bf16[512,3072]{1,0:T(8,128)(2,1)}, bf16[512,3072]{1,0:T(8,128)(2,1)}, bf16[2,24,128,128]{3,2,1,0:T(8,128)(2,1)}, f32[8,3072]{1,0:T(8,128)}) custom-call(f32[512,3072]{1,0:T(8,128)} %fusion.16.grad, bf16[512,3072]{1,0:T(8,128)(2,1)} %get-tuple-element.53.y_ref, bf16[512,3072]{1,0:T(8,128)(2,1)} %fusion.30.gate, f32[1,3072]{1,0:T(1,128)} %bitcast.405, ...), custom_call_target="tpu_custom_call" | custom-call | flops 402653184 | bytes 18874368 | tf_op jit(solution)/shard_map/gate_backward/pallas_call | solution.py:225
  924.5 30.9 %all_to_all.40 = bf16[96,64,128]{2,1,0:T(8,128)(2,1)S(1)} all-to-all(bf16[96,64,128]{2,1,0:T(8,128)(2,1)S(1)} %bitcast.382), channel_id=1, replica_groups=mesh['dp'=4,'seq'=8] {'seq'}, dimensions={0} | all-to-all | bytes 3145728 | tf_op jit(solution)/shard_map/all_to_all | solution.py:450
  957.0 26.5 %all_to_all.41 = bf16[96,64,128]{2,1,0:T(8,128)(2,1)} all-to-all(bf16[96,64,128]{2,1,0:T(8,128)(2,1)S(1)} %bitcast.379), channel_id=1, replica_groups=mesh['dp'=4,'seq'=8] {'seq'}, dimensions={0} | all-to-all | bytes 3145728 | tf_op jit(solution)/shard_map/all_to_all | solution.py:450
  983.5 93.0 %scan_backward.3 = (bf16[512,3376]{1,0:T(8,128)(2,1)}, f32[16,3328]{1,0:T(8,128)}, f32[16,3328]{1,0:T(8,128)}, f32[2,24,8,256]{3,2,1,0:T(8,128)}) custom-call(bf16[528,3376]{1,0:T(8,128)(2,1)} %copy-done, bf16[528,3376]{1,0:T(8,128)(2,1)} %copy-done, bf16[512,3072]{1,0:T(8,128)(2,1)} %get-tuple-element.55.grad, f32[8,3328]{1,0:T(8,128)} %get-tuple-element.187.par.par_bc, ...), custom_call_target="tpu_custom_call" | custom-call | flops 4026531840 | bytes 9437184 | tf_op jit(solution)/shard_map/scan_backward/pallas_call | solution.py:386
  1130.9 141.5 %reduce-scatter.7.cloned.1.call-done = bf16[48,3072]{1,0:T(8,128)(2,1)} async-done(((bf16[1536,3072]{1,0:T(8,128)(2,1)}), bf16[48,3072]{1,0:T(8,128)(2,1)}) %reduce-scatter.7.cloned.1.call-update) | async-done | bytes 294928 | tf_op jit(solution)/shard_map/reduce_scatter | solution.py:437
  1272.5 147.5 %reduce-scatter.13.cloned.1.call-done = bf16[48,3376]{1,0:T(8,128)(2,1)} async-done(((bf16[1536,3376]{1,0:T(8,128)(2,1)}), bf16[48,3376]{1,0:T(8,128)(2,1)}) %reduce-scatter.13.cloned.1.call-update) | async-done | bytes 324112 | tf_op jit(solution)/shard_map/reduce_scatter | solution.py:437
  1420.3 146.5 %reduce-scatter.9.cloned.1.call-done = bf16[48,3376]{1,0:T(8,128)(2,1)} async-done(((bf16[1536,3376]{1,0:T(8,128)(2,1)}), bf16[48,3376]{1,0:T(8,128)(2,1)}) %reduce-scatter.9.cloned.1.call-update) | async-done | bytes 324112 | tf_op jit(solution)/shard_map/reduce_scatter | solution.py:437
  1572.1 121.2 %all-reduce.4.cloned.1.call-done = f32[42789]{0:T(1024)} async-done(((f32[42789]{0:T(1024)}), f32[42789]{0:T(1024)}) %all-reduce.4.cloned.1.call-update) | async-done | bytes 171172 | tf_op jit(solution)/shard_map/psum | solution.py:636
  1702.5 23.6 %all-gather.33.cloned.1.call-done = bf16[768,1536]{1,0:T(8,128)(2,1)} async-done(((bf16[96,1536]{1,0:T(8,128)(2,1)}), bf16[768,1536]{1,0:T(8,128)(2,1)}) %all-gather.33.cloned.1.call-update) | async-done | bytes 2359312 | tf_op jit(solution)/shard_map/all_gather | solution.py:438
  1726.1 30.8 %all-gather.31.cloned.1.call-done = bf16[768,1536]{1,0:T(8,128)(2,1)} async-done(((bf16[96,1536]{1,0:T(8,128)(2,1)}), bf16[768,1536]{1,0:T(8,128)(2,1)}) %all-gather.31.cloned.1.call-update) | async-done | bytes 2359312 | tf_op jit(solution)/shard_map/all_gather | solution.py:438
  1763.6 24.1 %all-gather.27.cloned.1.call-done = bf16[384,3072]{1,0:T(8,128)(2,1)} async-done(((bf16[48,3072]{1,0:T(8,128)(2,1)}), bf16[384,3072]{1,0:T(8,128)(2,1)}) %all-gather.27.cloned.1.call-update) | async-done | bytes 2359312 | tf_op jit(solution)/shard_map/all_gather | solution.py:438
  1787.7 30.8 %all-gather.23.cloned.1.call-done = bf16[384,3072]{1,0:T(8,128)(2,1)} async-done(((bf16[48,3072]{1,0:T(8,128)(2,1)}), bf16[384,3072]{1,0:T(8,128)(2,1)}) %all-gather.23.cloned.1.call-update) | async-done | bytes 2359312 | tf_op jit(solution)/shard_map/all_gather | solution.py:438
  1818.4 32.0 %all-gather.29.cloned.1.call-done = bf16[384,3376]{1,0:T(8,128)(2,1)} async-done(((bf16[48,3376]{1,0:T(8,128)(2,1)}), bf16[384,3376]{1,0:T(8,128)(2,1)}) %all-gather.29.cloned.1.call-update) | async-done | bytes 2592784 | tf_op jit(solution)/shard_map/all_gather | solution.py:438
  1850.5 32.2 %all-gather.25.cloned.1.call-done = bf16[384,3376]{1,0:T(8,128)(2,1)} async-done(((bf16[48,3376]{1,0:T(8,128)(2,1)}), bf16[384,3376]{1,0:T(8,128)(2,1)}) %all-gather.25.cloned.1.call-update) | async-done | bytes 2592784 | tf_op jit(solution)/shard_map/all_gather | solution.py:438
  (406 shorter events, 517.7 us)
Async XLA Ops:
  7.2 97.1 %all-gather.35.cloned.1.call-start = ((), (), s32[]{:S(2)}) async-start(), calls=%async_computation.27 | async-start | bytes 10948608 | tf_op jit(solution)/shard_map/all_gather | solution.py:433
  14.6 191.4 %all-gather.37.cloned.1.call-start = ((), (), s32[]{:S(2)}) async-start(), calls=%async_computation.28 | async-start | bytes 9732096 | tf_op jit(solution)/shard_map/all_gather | solution.py:433
  20.3 272.6 %all-gather.39.cloned.1.call-start = ((), (), s32[]{:S(2)}) async-start(), calls=%async_computation.29 | async-start | bytes 9732096 | tf_op jit(solution)/shard_map/all_gather | solution.py:433
  25.2 356.2 %all-gather.41.cloned.1.call-start = ((), (), s32[]{:S(2)}) async-start(), calls=%async_computation.30 | async-start | bytes 10948608 | tf_op jit(solution)/shard_map/all_gather | solution.py:433
  26.7 463.1 %all-gather.45.cloned.1.call-start = ((), (), s32[]{:S(2)}) async-start(), calls=%async_computation.32 | async-start | bytes 9732096 | tf_op jit(solution)/shard_map/all_gather | solution.py:433
  28.5 534.6 %all-gather.43.cloned.1.call-start = ((), (), s32[]{:S(2)}) async-start(), calls=%async_computation.31 | async-start | bytes 9732096 | tf_op jit(solution)/shard_map/all_gather | solution.py:433
  30.0 49.9 %collective-permute-start = (f32[2,8,1536]{2,1,0:T(8,128)}, f32[2,8,1536]{2,1,0:T(8,128)S(1)}, u32[]{:S(2)}, u32[]{:S(2)}) collective-permute-start(f32[2,8,1536]{2,1,0:T(8,128)} %slice.460), channel_id=1, source_target_pairs={{0,1},{1,2},{2,3},{3,4},{4,5},{5,6},{6,7},{8,9},{9,10},{10,11},{11... | collective-permute-start | bytes 294920 | tf_op jit(solution)/shard_map/ppermute | solution.py:446
  159.4 36.0 %all-to-all-start = ((bf16[96,64,128]{2,1,0:T(8,128)(2,1)}), bf16[96,64,128]{2,1,0:T(8,128)(2,1)S(1)}, u32[]{:S(2)}, u32[]{:S(2)}) async-start(bf16[96,64,128]{2,1,0:T(8,128)(2,1)} %bitcast.381), calls=%async_computation | async-start | bytes 3145728 | tf_op jit(solution)/shard_map/all_to_all | solution.py:450
  201.7 26.7 %all-to-all-start.1 = ((bf16[96,64,128]{2,1,0:T(8,128)(2,1)}), bf16[96,64,128]{2,1,0:T(8,128)(2,1)S(1)}, u32[]{:S(2)}, u32[]{:S(2)}) async-start(bf16[96,64,128]{2,1,0:T(8,128)(2,1)} %bitcast.29), calls=%async_computation.1 | async-start | bytes 3145728 | tf_op jit(solution)/shard_map/all_to_all | solution.py:450
  441.4 30.3 %all-to-all-start.2 = ((bf16[96,64,128]{2,1,0:T(8,128)(2,1)}), bf16[96,64,128]{2,1,0:T(8,128)(2,1)}, u32[]{:S(2)}, u32[]{:S(2)}) async-start(bf16[96,64,128]{2,1,0:T(8,128)(2,1)} %bitcast.380), calls=%async_computation.2 | async-start | bytes 3145728 | tf_op jit(solution)/shard_map/all_to_all | solution.py:450
  485.5 86.8 %all-to-all-start.3 = ((bf16[96,64,128]{2,1,0:T(8,128)(2,1)}), bf16[96,64,128]{2,1,0:T(8,128)(2,1)}, u32[]{:S(2)}, u32[]{:S(2)}) async-start(bf16[96,64,128]{2,1,0:T(8,128)(2,1)} %bitcast.377), calls=%async_computation.3 | async-start | bytes 3145728 | tf_op jit(solution)/shard_map/all_to_all | solution.py:450
  641.7 480.1 %reduce-scatter.17.cloned.1.call-start = ((), (), s32[]{:S(2)}) async-start(), calls=%async_computation.25 | async-start | bytes 9732096 | tf_op jit(solution)/shard_map/reduce_scatter | solution.py:437
  676.5 445.8 %reduce-scatter.15.cloned.1.call-start = ((), (), s32[]{:S(2)}) async-start(), calls=%async_computation.23 | async-start | bytes 9732096 | tf_op jit(solution)/shard_map/reduce_scatter | solution.py:437
  840.2 290.6 %reduce-scatter.11.cloned.1.call-start = ((), (), s32[]{:S(2)}) async-start(), calls=%async_computation.19 | async-start | bytes 9732096 | tf_op jit(solution)/shard_map/reduce_scatter | solution.py:437
  851.1 421.3 %reduce-scatter.7.cloned.1.call-start = ((), (), s32[]{:S(2)}) async-start(), calls=%async_computation.15 | async-start | bytes 9732096 | tf_op jit(solution)/shard_map/reduce_scatter | solution.py:437
  910.9 509.1 %reduce-scatter.13.cloned.1.call-start = ((), (), s32[]{:S(2)}) async-start(), calls=%async_computation.21 | async-start | bytes 10948608 | tf_op jit(solution)/shard_map/reduce_scatter | solution.py:437
  923.1 643.8 %reduce-scatter.9.cloned.1.call-start = ((), (), s32[]{:S(2)}) async-start(), calls=%async_computation.17 | async-start | bytes 10948608 | tf_op jit(solution)/shard_map/reduce_scatter | solution.py:437
  1094.4 598.9 %all-reduce.4.cloned.1.call-start = ((), (), s32[]{:S(2)}) async-start(), calls=%async_computation.14 | async-start | bytes 344064 | tf_op jit(solution)/shard_map/psum | solution.py:636
  1121.7 604.4 %all-gather.33.cloned.1.call-start = ((), (), s32[]{:S(2)}) async-start(), calls=%async_computation.26 | async-start | bytes 2654208 | tf_op jit(solution)/shard_map/all_gather | solution.py:438
  1122.3 634.6 %all-gather.31.cloned.1.call-start = ((), (), s32[]{:S(2)}) async-start(), calls=%async_computation.24 | async-start | bytes 2654208 | tf_op jit(solution)/shard_map/all_gather | solution.py:438
  1122.9 664.8 %all-gather.27.cloned.1.call-start = ((), (), s32[]{:S(2)}) async-start(), calls=%async_computation.20 | async-start | bytes 2654208 | tf_op jit(solution)/shard_map/all_gather | solution.py:438
  1130.9 687.6 %all-gather.23.cloned.1.call-start = ((), (), s32[]{:S(2)}) async-start(), calls=%async_computation.16 | async-start | bytes 2654208 | tf_op jit(solution)/shard_map/all_gather | solution.py:438
  1272.4 578.0 %all-gather.29.cloned.1.call-start = ((), (), s32[]{:S(2)}) async-start(), calls=%async_computation.22 | async-start | bytes 2985984 | tf_op jit(solution)/shard_map/all_gather | solution.py:438
  1420.0 462.6 %all-gather.25.cloned.1.call-start = ((), (), s32[]{:S(2)}) async-start(), calls=%async_computation.18 | async-start | bytes 2985984 | tf_op jit(solution)/shard_map/all_gather | solution.py:438
  (73 other events, 1322.7 us)
Sparse Core Ops, SparseCore 0:
  14.7 89.5 all-gather.34
  107.2 92.7 all-gather.36
  202.9 89.8 all-gather.38
  295.6 85.6 all-gather.40
  384.1 81.8 all-gather.44
  468.8 94.3 all-gather.42
  651.2 135.5 reduce-scatter.16
  840.4 148.8 reduce-scatter.14
  995.8 135.0 reduce-scatter.10
  1137.6 134.7 reduce-scatter.6
  1279.1 140.8 reduce-scatter.12
  1425.9 140.8 reduce-scatter.8
  1572.4 120.8 all-reduce.3
  1695.1 30.9 all-gather.32
  1727.8 29.0 all-gather.30
  1758.6 29.0 all-gather.26
  1789.4 29.0 all-gather.22
  1820.2 30.2 all-gather.28
  1852.4 30.2 all-gather.24
